TPU v7x, 128 devices: a whole 4x4x4 slice. The times are simulated.
128 devices in a mesh: grp: 16 (over x, y), blk: 8 (over z, core).
Axes of the slice: x: 4, y: 4, z: 4, core: 2. Of those that a mesh axis runs over, the one named last changes fastest.
Arguments:
- visual: bfloat16 [98304, 3584], P(('grp', 'blk')), may hold values from -6 to 6
- text_queries: float32 [4096, 3584], P(('grp', 'blk')), may hold values from -100 to 100
- kv_weight: bfloat16 [3584, 1024], replicated, may hold values from -0.09375 to 0.09375
- placement: int32 [12288, 1], P(('grp', 'blk')), may hold values from 0 to 127; in each aligned block of 96 rows (0 to 95, 96 to 191, ...) at most 2 rows name the same one
Outputs:
- attended: float32 [4096, 3584], P(('grp', 'blk'))
Inputs may be any that keep to these rules, and one draw needn't show every extreme that they name: `placement`: among the 96 blocks of one frame owner at most 2 name the same attention owner, a bound that some block reaches; every attention owner is named by some block.
All inputs are finite; a program needn't handle non-finite values.
Results may differ from a plain program's by a relative error of at most 0.0003.
Values sent between devices are 32-bit elements; how exact they have to be, the bound alone decides.
No kernel may reach another device: no remote copies, remote signals or barrier semaphores. Data moves between devices by JAX's collectives and lax.ppermute only.
A program may use at most 128 MiB of HBM per device.

v0:
```python
import jax
import jax.numpy as jnp
from jax import lax
from jax.sharding import PartitionSpec as P

HEADS = 28
KV_HEADS = 4


def copy_for_each(shard, axis):
    devices = lax.axis_size(axis)
    return lax.all_to_all(
        jnp.broadcast_to(shard[None], (devices, *shard.shape)), axis, 0, 0, tiled=True
    )


def over_copies(shard, axis):
    everything = copy_for_each(shard, axis)
    return jnp.max(everything, axis=0)


def split_up(shard, dim, devices):
    before, after = (shard.shape[:dim], shard.shape[dim + 1 :])
    return jnp.moveaxis(shard.reshape(*before, devices, -1, *after), dim, 0)


def sent_and_summed(shard, axis, dim):
    pieces = split_up(shard, dim, lax.axis_size(axis))
    arrived = lax.all_to_all(pieces, axis, split_axis=0, concat_axis=0, tiled=True)
    return arrived.sum(axis=0)


def sent_together(arrays, axis, dim, along):
    columns = [a.reshape(*a.shape[:along], -1) for a in arrays]
    both = jnp.concatenate(columns, axis=along)
    whole, at, outs = (sent_and_summed(both, axis, dim), 0, [])
    for a, column in zip(arrays, columns):
        share = whole[..., at : at + column.shape[along]]
        outs.append(share.reshape(*share.shape[:along], *a.shape[along:]))
        at += column.shape[along]
    return tuple(outs)


def attend(state, keys_all, valid):
    queries, output, peak, total = state
    nkeys = keys_all.shape[0]
    heads_kv = queries.shape[1]
    head_dim = queries.shape[3]
    stride = min(512, nkeys)
    scale = head_dim ** (-0.5)

    def visit(turn, carry):
        output, peak, total = carry
        start = turn * stride
        piece = lax.dynamic_slice_in_dim(keys_all, start, stride, 0)
        marks = lax.dynamic_slice_in_dim(valid, start, stride, 0) > 0.5
        key_heads = piece[:, : heads_kv * head_dim].reshape(stride, heads_kv, head_dim)
        value_heads = piece[:, heads_kv * head_dim :].reshape(stride, heads_kv, head_dim)
        scores = (
            jnp.einsum("rgjd,kgd->rgjk", queries, key_heads, precision=lax.Precision.HIGHEST)
            * scale
        )
        scores = jnp.where(marks[None, None, None, :], scores, -1e30)
        fresh = jnp.maximum(peak, jnp.max(scores, axis=-1))
        weights = jnp.where(marks[None, None, None, :], jnp.exp(scores - fresh[..., None]), 0.0)
        factor = jnp.exp(peak - fresh)
        total = total * factor + jnp.sum(weights, axis=-1)
        output = output * factor[..., None] + jnp.einsum(
            "rgjk,kgd->rgjd", weights, value_heads, precision=lax.Precision.HIGHEST
        )
        return (output, fresh, total)

    output, peak, total = lax.fori_loop(0, nkeys // stride, visit, (output, peak, total))
    return (queries, output, peak, total)


def start_state(queries):
    return (
        queries,
        jnp.zeros_like(queries),
        jnp.full(queries.shape[:3], -1e30, jnp.float32),
        jnp.zeros(queries.shape[:3], jnp.float32),
    )


def on_device(visual, text_queries, kv_weight, placement):
    kv = jnp.dot(visual, kv_weight, preferred_element_type=jnp.float32)
    width = kv.shape[1]
    head_dim = width // (2 * KV_HEADS)
    group = HEADS // KV_HEADS
    blocks = placement.shape[0]
    block_rows = kv.shape[0] // blocks
    groups_count = lax.axis_size("grp")
    cycle_size = lax.axis_size("blk")
    devices = groups_count * cycle_size
    per_pair = max(2, blocks // devices + 1)
    owner = placement[:, 0]
    index = jnp.arange(blocks, dtype=jnp.int32)
    earlier = (owner[:, None] == owner[None, :]) & (index[None, :] < index[:, None])
    rank = jnp.sum(earlier.astype(jnp.int32), axis=1, dtype=jnp.int32)
    slot = owner * per_pair + rank
    outgoing = (
        jnp.zeros((devices * per_pair, block_rows * width), jnp.float32)
        .at[slot]
        .set(kv.reshape(blocks, block_rows * width))
    )
    marks = jnp.zeros((devices * per_pair, block_rows), jnp.float32).at[slot].set(1.0)
    outgoing = outgoing.reshape(devices, per_pair * block_rows, width)
    marks = marks.reshape(devices, per_pair * block_rows)
    arrived, arrived_marks = (
        lax.all_to_all(outgoing, ("grp", "blk"), split_axis=0, concat_axis=0, tiled=True),
        lax.all_to_all(marks, ("grp", "blk"), split_axis=0, concat_axis=0, tiled=True),
    )
    keys_all = arrived.reshape(-1, width)
    valid = arrived_marks.reshape(-1)
    rows = text_queries.shape[0]
    gathered = lax.all_gather(text_queries, "blk", axis=0, tiled=True)
    every = gathered.shape[0]
    state = attend(start_state(gathered.reshape(every, KV_HEADS, group, head_dim)), keys_all, valid)
    local_out, local_peak, local_total = (state[1], state[2], state[3])
    global_peak = over_copies(local_peak, "blk")
    factor = jnp.exp(local_peak - global_peak)
    output, total = sent_together(
        (local_out * factor[..., None], local_total * factor), "blk", 0, 3
    )
    attended = output / total[..., None]
    return attended.reshape(rows, HEADS * head_dim)


def solution(mesh):
    placed = (P(("grp", "blk"), None), P(("grp", "blk"), None), P(), P(("grp", "blk"), None))
    return jax.shard_map(
        on_device, mesh=mesh, in_specs=placed, out_specs=P(("grp", "blk"), None), check_vma=False
    )
```

profile of v0, /device:TPU:16, one launch (start us, length us, event | category | flops | bytes accessed | tf_op | source)
XLA Modules:
  0.0 482.5 jit_solution(4864615598852005550)
XLA Ops:
  6.5 0.9 convert_reduce_fusion
  7.4 0.7 fusion.23
  8.1 0.8 scatter_custom_fusion
  9.0 0.7 all_to_all.15
  9.7 10.3 %all-to-all-start = ((f32[128,1,16]{2,1,0:T(1,128)}), f32[128,1,16]{2,1,0:T(1,128)S(1)}, u32[]{:S(2)}, u32[]{:S(2)}) async-start(f32[128,1,16]{2,1,0:T(1,128)} %bitcast.3), calls=%async_computation | async-start | bytes 131072 | tf_op jit(solution)/shard_map/all_to_all | solution.py:112
  20.0 10.9 %fusion.24 = f32[768,1024]{1,0:T(8,128)} fusion(bf16[768,3584]{1,0:T(8,128)(2,1)} %param.6, bf16[3584,1024]{1,0:T(8,128)(2,1)} %param.8), kind=kOutput, calls=%fused_computation.42 | convolution fusion | flops 5637144576 | bytes 15990784 | tf_op jit(solution)/shard_map/dot_general | solution.py:87
  30.9 2.9 reshape.67
  33.8 6.0 %scatter_custom_fusion.1 = f32[256,8192]{1,0:T(8,128)} fusion(s32[96]{0:T(128)S(1)} %fusion.23, f32[96,8192]{1,0:T(8,128)S(1)} %reshape.67, f32[]{:T(128)} %constant.71.clone.1), kind=kCustom, calls=%fused_computation.27 | custom fusion | bytes 8388612 | tf_op jit(solution)/shard_map/scatter | solution.py:105
  39.8 9.4 %reshape.51 = f32[128,16,1024]{2,1,0:T(8,128)} reshape(f32[256,8192]{1,0:T(8,128)} %scatter_custom_fusion.1) | data formatting | bytes 16777216 | tf_op jit(solution)/shard_map/reshape | solution.py:108
  49.2 10.2 %all-to-all-start.1 = ((f32[128,16,1024]{2,1,0:T(8,128)}), f32[128,16,1024]{2,1,0:T(8,128)}, u32[]{:S(2)}, u32[]{:S(2)}) async-start(f32[128,16,1024]{2,1,0:T(8,128)} %reshape.51), calls=%async_computation.1 | async-start | bytes 16777216 | tf_op jit(solution)/shard_map/all_to_all | solution.py:111
  59.5 0.7 all-gather.2.cloned.1.call-update
  60.2 0.5 broadcast.74
  60.7 0.7 reduce.3
  61.5 113.6 %all-gather.2.cloned.1.call-done = f32[256,3584]{1,0:T(8,128)} async-done(((f32[32,3584]{1,0:T(8,128)}), f32[256,3584]{1,0:T(8,128)}) %all-gather.2.cloned.1.call-update) | async-done | bytes 3670032 | tf_op jit(solution)/shard_map/all_gather | solution.py:117
  175.1 5.1 %copy.54 = f32[256,3584]{0,1:T(8,128)} copy(f32[256,3584]{1,0:T(8,128)} %all-gather.2.cloned.1.call-done) | data formatting | bytes 7340032 | tf_op jit(solution)/shard_map/all_gather | solution.py:117
  180.3 4.6 copy.56
  184.9 177.2 %while.18 = (s32[]{:T(128)}, f32[256,4,7,128]{0,3,2,1:T(8,128)}, f32[256,4,7]{0,2,1:T(8,128)S(1)}, f32[256,4,7]{0,2,1:T(8,128)S(1)}, f32[2048]{0:T(1024)S(1)}, /...) while((s32[]{:T(128)}, f32[256,4,7,128]{0,3,2,1:T(8,128)}, ...), condition=%wide.region_6.7_spmd.clone, body=%wide.region_3.6_spmd.clone.sunk | while | flops 11321118720 | bytes 95359232 | solution.py:73
  204.5 1.7 constant_dynamic-slice_fusion.2
  206.9 18.3 %bitcast_reduce_fusion.2 = (f32[256,4,7]{0,2,1:T(8,128)S(1)}, f32[4,512,256,7]{2,1,3,0:T(8,128)S(1)}) fusion(pred[512]{0:T(512)(128)(4,1)S(1)} %dynamic-slice_compare_fusion.2, f32[512,4,128,1]{0,2,3,1:T(8,128)S(1)} %bitcast.63, f32[256,4,7,128]{3,0,2,1:T(8,128)} %get-tuple-element.293), kind=kOutput, calls=%fused_computation.3.clone.1 | convolution fusion | flops 5648147456 | bytes 19427840 | tf_op jit(solution)/shard_map/while/body/eval_jaxpr/rgjd,kgd->rgjk/dot_general | solution.py:60
  225.3 4.0 fusion.40
  229.4 12.6 %bitcast_add_fusion.3 = f32[256,4,7,128]{0,3,2,1:T(8,128)S(1)} fusion(f32[256,4,7,128]{0,3,2,1:T(8,128)S(1)} %copy-done.1, f32[512,4,128,1]{0,2,3,1:T(8,128)S(1)} %bitcast.64, f32[4,512,256,7]{2,1,3,0:T(8,128)S(1)} %get-tuple-element.259, f32[256,4,7]{0,2,1:T(8,128)S(1)} %select_maximum_fusion.2, pred[512]{0:T(512)(128)(4,1)S(1)} %dynamic-slice_compare_fusion.2, ...), kind=kOutput, calls=%fused_computation.15.clone.1 | convolution fusion | flops 5654577152 | bytes 23126528 | tf_op jit(solution)/shard_map/while/body/eval_jaxpr/rgjk,kgd->rgjd/dot_general | solution.py:68
  242.0 1.8 copy-done.2
  243.9 1.7 constant_dynamic-slice_fusion.2
  246.3 18.3 %bitcast_reduce_fusion.2 = (f32[256,4,7]{0,2,1:T(8,128)S(1)}, f32[4,512,256,7]{2,1,3,0:T(8,128)S(1)}) fusion(pred[512]{0:T(512)(128)(4,1)S(1)} %dynamic-slice_compare_fusion.2, f32[512,4,128,1]{0,2,3,1:T(8,128)S(1)} %bitcast.63, f32[256,4,7,128]{3,0,2,1:T(8,128)} %get-tuple-element.293), kind=kOutput, calls=%fused_computation.3.clone.1 | convolution fusion | flops 5648147456 | bytes 19427840 | tf_op jit(solution)/shard_map/while/body/eval_jaxpr/rgjd,kgd->rgjk/dot_general | solution.py:60
  264.7 4.0 fusion.40
  268.7 12.6 %bitcast_add_fusion.3 = f32[256,4,7,128]{0,3,2,1:T(8,128)S(1)} fusion(f32[256,4,7,128]{0,3,2,1:T(8,128)S(1)} %copy-done.1, f32[512,4,128,1]{0,2,3,1:T(8,128)S(1)} %bitcast.64, f32[4,512,256,7]{2,1,3,0:T(8,128)S(1)} %get-tuple-element.259, f32[256,4,7]{0,2,1:T(8,128)S(1)} %select_maximum_fusion.2, pred[512]{0:T(512)(128)(4,1)S(1)} %dynamic-slice_compare_fusion.2, ...), kind=kOutput, calls=%fused_computation.15.clone.1 | convolution fusion | flops 5654577152 | bytes 23126528 | tf_op jit(solution)/shard_map/while/body/eval_jaxpr/rgjk,kgd->rgjd/dot_general | solution.py:68
  281.3 1.8 copy-done.2
  283.2 1.7 constant_dynamic-slice_fusion.2
  285.6 18.3 %bitcast_reduce_fusion.2 = (f32[256,4,7]{0,2,1:T(8,128)S(1)}, f32[4,512,256,7]{2,1,3,0:T(8,128)S(1)}) fusion(pred[512]{0:T(512)(128)(4,1)S(1)} %dynamic-slice_compare_fusion.2, f32[512,4,128,1]{0,2,3,1:T(8,128)S(1)} %bitcast.63, f32[256,4,7,128]{3,0,2,1:T(8,128)} %get-tuple-element.293), kind=kOutput, calls=%fused_computation.3.clone.1 | convolution fusion | flops 5648147456 | bytes 19427840 | tf_op jit(solution)/shard_map/while/body/eval_jaxpr/rgjd,kgd->rgjk/dot_general | solution.py:60
  304.0 4.0 fusion.40
  308.1 12.6 %bitcast_add_fusion.3 = f32[256,4,7,128]{0,3,2,1:T(8,128)S(1)} fusion(f32[256,4,7,128]{0,3,2,1:T(8,128)S(1)} %copy-done.1, f32[512,4,128,1]{0,2,3,1:T(8,128)S(1)} %bitcast.64, f32[4,512,256,7]{2,1,3,0:T(8,128)S(1)} %get-tuple-element.259, f32[256,4,7]{0,2,1:T(8,128)S(1)} %select_maximum_fusion.2, pred[512]{0:T(512)(128)(4,1)S(1)} %dynamic-slice_compare_fusion.2, ...), kind=kOutput, calls=%fused_computation.15.clone.1 | convolution fusion | flops 5654577152 | bytes 23126528 | tf_op jit(solution)/shard_map/while/body/eval_jaxpr/rgjk,kgd->rgjd/dot_general | solution.py:68
  320.7 1.8 copy-done.2
  322.6 1.7 constant_dynamic-slice_fusion.2
  325.0 18.3 %bitcast_reduce_fusion.2 = (f32[256,4,7]{0,2,1:T(8,128)S(1)}, f32[4,512,256,7]{2,1,3,0:T(8,128)S(1)}) fusion(pred[512]{0:T(512)(128)(4,1)S(1)} %dynamic-slice_compare_fusion.2, f32[512,4,128,1]{0,2,3,1:T(8,128)S(1)} %bitcast.63, f32[256,4,7,128]{3,0,2,1:T(8,128)} %get-tuple-element.293), kind=kOutput, calls=%fused_computation.3.clone.1 | convolution fusion | flops 5648147456 | bytes 19427840 | tf_op jit(solution)/shard_map/while/body/eval_jaxpr/rgjd,kgd->rgjk/dot_general | solution.py:60
  343.3 4.0 fusion.40
  347.4 12.6 %bitcast_add_fusion.3 = f32[256,4,7,128]{0,3,2,1:T(8,128)S(1)} fusion(f32[256,4,7,128]{0,3,2,1:T(8,128)S(1)} %copy-done.1, f32[512,4,128,1]{0,2,3,1:T(8,128)S(1)} %bitcast.64, f32[4,512,256,7]{2,1,3,0:T(8,128)S(1)} %get-tuple-element.259, f32[256,4,7]{0,2,1:T(8,128)S(1)} %select_maximum_fusion.2, pred[512]{0:T(512)(128)(4,1)S(1)} %dynamic-slice_compare_fusion.2, ...), kind=kOutput, calls=%fused_computation.15.clone.1 | convolution fusion | flops 5654577152 | bytes 23126528 | tf_op jit(solution)/shard_map/while/body/eval_jaxpr/rgjk,kgd->rgjd/dot_general | solution.py:68
  360.0 1.8 copy-done.2
  362.1 0.7 broadcast_in_dim.81
  362.8 3.4 all-to-all-start.2
  366.2 4.6 copy.60
  370.8 2.5 all-to-all-done.2
  373.5 2.8 copy.62
  376.3 2.8 broadcast_multiply_fusion
  379.4 0.9 pad_maximum_fusion
  380.3 1.4 copy.63
  381.7 87.9 %all_to_all.24 = f32[8,32,4,7,129]{4,1,3,2,0:T(8,128)} all-to-all(f32[8,32,4,7,129]{4,1,3,2,0:T(8,128)S(1)} %copy.63), channel_id=1, replica_groups=mesh['grp'=16,'blk'=8] {'blk'}, dimensions={0} | all-to-all | bytes 7397376 | tf_op jit(solution)/shard_map/all_to_all | solution.py:29
  469.6 4.0 reduce_sum.35
  474.4 0.9 reshape.54
  (55 shorter events, 4.6 us)
Async XLA Ops:
  9.7 39.5 %all-to-all-start = ((f32[128,1,16]{2,1,0:T(1,128)}), f32[128,1,16]{2,1,0:T(1,128)S(1)}, u32[]{:S(2)}, u32[]{:S(2)}) async-start(f32[128,1,16]{2,1,0:T(1,128)} %bitcast.3), calls=%async_computation | async-start | bytes 131072 | tf_op jit(solution)/shard_map/all_to_all | solution.py:112
  49.2 135.7 %all-to-all-start.1 = ((f32[128,16,1024]{2,1,0:T(8,128)}), f32[128,16,1024]{2,1,0:T(8,128)}, u32[]{:S(2)}, u32[]{:S(2)}) async-start(f32[128,16,1024]{2,1,0:T(8,128)} %reshape.51), calls=%async_computation.1 | async-start | bytes 16777216 | tf_op jit(solution)/shard_map/all_to_all | solution.py:111
  59.4 115.7 %all-gather.2.cloned.1.call-start = ((), (), s32[]{:S(2)}) async-start(), calls=%async_computation.4 | async-start | bytes 4128768 | tf_op jit(solution)/shard_map/all_gather | solution.py:117
  225.3 4.1 copy-start.1
  242.0 1.8 copy-start.2
  264.6 4.1 copy-start.1
  281.3 1.8 copy-start.2
  304.0 4.1 copy-start.1
  320.7 1.8 copy-start.2
  343.3 4.1 copy-start.1
  360.0 1.8 copy-start.2
  362.8 10.5 %all-to-all-start.2 = ((f32[8,256,4,7]{1,2,3,0:T(4,128)}), f32[8,256,4,7]{1,2,3,0:T(4,128)S(1)}, u32[]{:S(2)}, u32[]{:S(2)}) async-start(f32[8,256,4,7]{1,2,3,0:T(4,128)} %broadcast_in_dim.81), calls=%async_computation.2 | async-start | bytes 458752 | tf_op jit(solution)/shard_map/all_to_all | solution.py:12
  376.3 3.1 copy-start
Sparse Core Ops, SparseCore 0:
  61.9 113.1 all-gather.1
where the time goes:
time: 489 us; the launch traced here: 483 us
  matrix products  135 us (28%)
  waiting for transfers between devices  117 us (24%)
  blocking collectives  87.9 us (18%)
  local copies, waits for them, and re-layouts  58.3 us (12%)
  other arithmetic  26.8 us (5%)
  starting transfers between devices  24 us (5%)
  loops' own time  20.1 us (4%)
  between operations  14 us (3%)
    all_gather x1, waiting for transfers between devices, on_device(): gathered = lax.all_gather(text_queries, 'blk', axis=0, tiled=True)  114 us
    all_to_all x1, blocking collectives, sent_and_summed(): lax.all_to_all(pieces, axis, split_axis=0, concat_axis=0, tiled=True)  87.9 us
    dot_general x4, matrix products, visit(): jnp.einsum('rgjd,kgd->rgjk', queries, key_heads, precision=lax.Precision....  73.4 us
    dot_general x4, matrix products, visit(): jnp.einsum('rgjk,kgd->rgjd', weights, value_heads, precision=lax.Precisio...  50.4 us
    another operation x1, loops' own time, attend(): lax.fori_loop(0, nkeys // stride, visit, (output, peak, total))  20.1 us
    reduce_sum x4, other arithmetic, visit(): total = total * factor + jnp.sum(weights, axis=-1)  16.1 us
    dot_general x1, matrix products, on_device(): kv = jnp.dot(visual, kv_weight, preferred_element_type=jnp.float32)  10.9 us
    all_to_all x1, starting transfers between devices, on_device(): lax.all_to_all(marks, ('grp', 'blk'), split_axis=0, concat_axis=0, tiled=...  10.3 us
  transfers between devices with their start and end apart: 4, of which 2 were waited for; matrix products, arithmetic and copies ran while one was open for 9% of the time, Pallas kernels for 0%

commit v1 on v0

--- a/solution.py
+++ b/solution.py
@@ -114,7 +114,16 @@
     keys_all = arrived.reshape(-1, width)
     valid = arrived_marks.reshape(-1)
     rows = text_queries.shape[0]
-    gathered = lax.all_gather(text_queries, "blk", axis=0, tiled=True)
+    ways = lax.axis_size("blk")
+    up = [(d, (d + 1) % ways) for d in range(ways)]
+    down = [(d, (d - 1) % ways) for d in range(ways)]
+    earlier_2, later = ([text_queries], [text_queries])
+    for _ in range(ways // 2):
+        earlier_2.append(lax.ppermute(earlier_2[-1], "blk", up))
+    for _ in range((ways - 1) // 2):
+        later.append(lax.ppermute(later[-1], "blk", down))
+    line = jnp.concatenate([*earlier_2[::-1], *later[1:]], axis=0)
+    gathered = jnp.roll(line, (lax.axis_index("blk") - ways // 2) * text_queries.shape[0], axis=0)
     every = gathered.shape[0]
     state = attend(start_state(gathered.reshape(every, KV_HEADS, group, head_dim)), keys_all, valid)
     local_out, local_peak, local_total = (state[1], state[2], state[3])

time: 489 us -> 523 us (1.070)
  the two profiles are of different devices: /device:TPU:16 before, /device:TPU:10 now
where the time goes in v1:
time: 523 us; the launch traced here: 513 us
  matrix products  135 us (26%)
  waiting for transfers between devices  102 us (20%)
  local copies, waits for them, and re-layouts  97.2 us (19%)
  blocking collectives  87.9 us (17%)
  starting transfers between devices  44.3 us (8%)
  other arithmetic  26.8 us (5%)
  loops' own time  20.1 us (4%)
    ppermute x4, waiting for transfers between devices, on_device(): earlier_2.append(lax.ppermute(earlier_2[-1], 'blk', up))  99 us
    all_to_all x1, blocking collectives, sent_and_summed(): lax.all_to_all(pieces, axis, split_axis=0, concat_axis=0, tiled=True)  87.9 us
    dot_general x4, matrix products, visit(): jnp.einsum('rgjd,kgd->rgjk', queries, key_heads, precision=lax.Precision....  73.4 us
    dot_general x4, matrix products, visit(): jnp.einsum('rgjk,kgd->rgjd', weights, value_heads, precision=lax.Precisio...  50.4 us
    concatenate x1, local copies, waits for them, and re-layouts, on_device(): jnp.roll(line, (lax.axis_index('blk') - ways // 2) * text_queries.shape[0...  20.2 us
    another operation x1, loops' own time, attend(): lax.fori_loop(0, nkeys // stride, visit, (output, peak, total))  20.1 us
    reduce_sum x4, other arithmetic, visit(): total = total * factor + jnp.sum(weights, axis=-1)  16.1 us
    ppermute x4, starting transfers between devices, on_device(): earlier_2.append(lax.ppermute(earlier_2[-1], 'blk', up))  11.2 us
  transfers between devices with their start and end apart: 10, of which 4 were waited for; matrix products, arithmetic and copies ran while one was open for 16% of the time, Pallas kernels for 0%

profile of v1, /device:TPU:10, one launch (start us, length us, event | category | flops | bytes accessed | tf_op | source)
XLA Modules:
  0.0 513.1 jit_solution(14654791834145981433)
XLA Ops:
  3.1 10.4 %all-to-all-start = ((f32[128,1,16]{2,1,0:T(1,128)}), f32[128,1,16]{2,1,0:T(1,128)S(1)}, u32[]{:S(2)}, u32[]{:S(2)}) async-start(f32[128,1,16]{2,1,0:T(1,128)} %bitcast.3), calls=%async_computation | async-start | bytes 131072 | tf_op jit(solution)/shard_map/all_to_all | solution.py:112
  13.6 10.9 %fusion.24 = f32[768,1024]{1,0:T(8,128)} fusion(bf16[768,3584]{1,0:T(8,128)(2,1)} %param.6, bf16[3584,1024]{1,0:T(8,128)(2,1)} %param.8), kind=kOutput, calls=%fused_computation.43 | convolution fusion | flops 5637144576 | bytes 15990784 | tf_op jit(solution)/shard_map/dot_general | solution.py:87
  24.5 2.9 reshape.67
  27.4 6.0 %scatter_custom_fusion.1 = f32[256,8192]{1,0:T(8,128)} fusion(s32[96]{0:T(128)S(1)} %fusion.23, f32[96,8192]{1,0:T(8,128)S(1)} %reshape.67, f32[]{:T(128)} %constant.95.clone.1), kind=kCustom, calls=%fused_computation.27 | custom fusion | bytes 8388612 | tf_op jit(solution)/shard_map/scatter | solution.py:105
  33.3 9.4 %reshape.51 = f32[128,16,1024]{2,1,0:T(8,128)} reshape(f32[256,8192]{1,0:T(8,128)} %scatter_custom_fusion.1) | data formatting | bytes 16777216 | tf_op jit(solution)/shard_map/reshape | solution.py:108
  42.7 10.2 %all-to-all-start.1 = ((f32[128,16,1024]{2,1,0:T(8,128)}), f32[128,16,1024]{2,1,0:T(8,128)}, u32[]{:S(2)}, u32[]{:S(2)}) async-start(f32[128,16,1024]{2,1,0:T(8,128)} %reshape.51), calls=%async_computation.1 | async-start | bytes 16777216 | tf_op jit(solution)/shard_map/all_to_all | solution.py:111
  53.1 3.0 collective-permute-start.4
  56.2 90.1 %collective-permute-done = f32[32,3584]{1,0:T(8,128)S(1)} collective-permute-done((f32[32,3584]{1,0:T(8,128)S(1)}, f32[32,3584]{1,0:T(8,128)S(1)}, u32[]{:S(2)}, u32[]{:S(2)}) %collective-permute-start) | collective-permute-done | bytes 458784 | tf_op jit(solution)/shard_map/ppermute | solution.py:122
  146.2 6.2 %collective-permute-start.1 = (f32[32,3584]{1,0:T(8,128)S(1)}, f32[32,3584]{1,0:T(8,128)S(1)}, u32[]{:S(2)}, u32[]{:S(2)}) collective-permute-start(f32[32,3584]{1,0:T(8,128)S(1)} %collective-permute-done), channel_id=1, source_target_pairs={{0,1},{1,2},{2,3},{3,4},{4,5},{5,6},{6,7},{7,0},{8,9},{9,10},{10,1... | collective-permute-start | bytes 1376264 | tf_op jit(solution)/shard_map/ppermute | solution.py:122
  152.4 4.8 collective-permute-done.1
  157.2 3.1 collective-permute-start.2
  160.3 2.0 collective-permute-start.6
  162.4 4.1 collective-permute-done.2
  166.5 1.8 collective-permute-start.3
  170.2 2.8 copy.92
  173.0 1.8 copy.90
  174.8 2.8 copy.93
  177.6 1.8 copy.89
  179.3 2.8 copy.88
  182.2 2.8 copy.94
  185.0 2.8 copy.87
  187.8 20.2 %concatenate.14 = f32[512,3584]{0,1:T(8,128)} concatenate(f32[32,3584]{0,1:T(8,128)} %copy.87, f32[32,3584]{0,1:T(8,128)} %copy.88, f32[32,3584]{0,1:T(8,128)} %copy.89, f32[32,3584]{0,1:T(8,128)} %copy.90, f32[32,3584]{0,1:T(8,128)S(1)} %copy.91, f32[32,3584]{0,1:T(8,128)} %copy.92, f32[32,3584]{0,1:T(8,128)} %copy.93, f32[32,3584]{0,1:T(8,128)} %copy.94, f32[32,3584]{0,1:T(8,128)} %copy.87, ...), dimensions={0} | concatenate | bytes 14680064 | tf_op jit(solution)/shard_map/jit(_roll_dynamic)/concatenate | solution.py:126
  208.0 5.5 %constant_dynamic-slice_fusion.1 = f32[256,3584]{0,1:T(8,128)} fusion(f32[512,3584]{0,1:T(8,128)} %concatenate.14, s32[]{:T(128)S(6)} %select_n.46), kind=kLoop, calls=%fused_computation.42 | loop fusion | bytes 7340036 | tf_op jit(solution)/shard_map/jit(_roll_dynamic)/dynamic_slice | solution.py:126
  213.5 4.6 copy.104
  218.1 177.4 %while.18 = (s32[]{:T(128)}, f32[256,4,7,128]{0,3,2,1:T(8,128)}, f32[256,4,7]{0,2,1:T(8,128)S(1)}, f32[256,4,7]{0,2,1:T(8,128)S(1)}, f32[2048]{0:T(1024)S(1)}, /...) while((s32[]{:T(128)}, f32[256,4,7,128]{0,3,2,1:T(8,128)}, ...), condition=%wide.region_6.7_spmd.clone, body=%wide.region_3.6_spmd.clone.sunk | while | flops 11321118720 | bytes 95359232 | solution.py:73
  240.2 18.3 %bitcast_reduce_fusion.2 = (f32[256,4,7]{0,2,1:T(8,128)S(1)}, f32[4,512,256,7]{2,1,3,0:T(8,128)S(1)}) fusion(pred[512]{0:T(512)(128)(4,1)S(1)} %dynamic-slice_compare_fusion.2, f32[512,4,128,1]{0,2,3,1:T(8,128)S(1)} %bitcast.63, f32[256,4,7,128]{3,0,2,1:T(8,128)} %get-tuple-element.293), kind=kOutput, calls=%fused_computation.3.clone.1 | convolution fusion | flops 5648147456 | bytes 19427840 | tf_op jit(solution)/shard_map/while/body/eval_jaxpr/rgjd,kgd->rgjk/dot_general | solution.py:60
  258.5 4.0 fusion.40
  262.6 12.6 %bitcast_add_fusion.3 = f32[256,4,7,128]{0,3,2,1:T(8,128)S(1)} fusion(f32[256,4,7,128]{0,3,2,1:T(8,128)S(1)} %copy-done.1, f32[512,4,128,1]{0,2,3,1:T(8,128)S(1)} %bitcast.64, f32[4,512,256,7]{2,1,3,0:T(8,128)S(1)} %get-tuple-element.259, f32[256,4,7]{0,2,1:T(8,128)S(1)} %select_maximum_fusion.2, pred[512]{0:T(512)(128)(4,1)S(1)} %dynamic-slice_compare_fusion.2, ...), kind=kOutput, calls=%fused_computation.15.clone.1 | convolution fusion | flops 5654577152 | bytes 23126528 | tf_op jit(solution)/shard_map/while/body/eval_jaxpr/rgjk,kgd->rgjd/dot_general | solution.py:68
  275.2 1.9 copy-done.2
  279.6 18.3 %bitcast_reduce_fusion.2 = (f32[256,4,7]{0,2,1:T(8,128)S(1)}, f32[4,512,256,7]{2,1,3,0:T(8,128)S(1)}) fusion(pred[512]{0:T(512)(128)(4,1)S(1)} %dynamic-slice_compare_fusion.2, f32[512,4,128,1]{0,2,3,1:T(8,128)S(1)} %bitcast.63, f32[256,4,7,128]{3,0,2,1:T(8,128)} %get-tuple-element.293), kind=kOutput, calls=%fused_computation.3.clone.1 | convolution fusion | flops 5648147456 | bytes 19427840 | tf_op jit(solution)/shard_map/while/body/eval_jaxpr/rgjd,kgd->rgjk/dot_general | solution.py:60
  298.0 4.0 fusion.40
  302.0 12.6 %bitcast_add_fusion.3 = f32[256,4,7,128]{0,3,2,1:T(8,128)S(1)} fusion(f32[256,4,7,128]{0,3,2,1:T(8,128)S(1)} %copy-done.1, f32[512,4,128,1]{0,2,3,1:T(8,128)S(1)} %bitcast.64, f32[4,512,256,7]{2,1,3,0:T(8,128)S(1)} %get-tuple-element.259, f32[256,4,7]{0,2,1:T(8,128)S(1)} %select_maximum_fusion.2, pred[512]{0:T(512)(128)(4,1)S(1)} %dynamic-slice_compare_fusion.2, ...), kind=kOutput, calls=%fused_computation.15.clone.1 | convolution fusion | flops 5654577152 | bytes 23126528 | tf_op jit(solution)/shard_map/while/body/eval_jaxpr/rgjk,kgd->rgjd/dot_general | solution.py:68
  314.6 1.9 copy-done.2
  319.0 18.3 %bitcast_reduce_fusion.2 = (f32[256,4,7]{0,2,1:T(8,128)S(1)}, f32[4,512,256,7]{2,1,3,0:T(8,128)S(1)}) fusion(pred[512]{0:T(512)(128)(4,1)S(1)} %dynamic-slice_compare_fusion.2, f32[512,4,128,1]{0,2,3,1:T(8,128)S(1)} %bitcast.63, f32[256,4,7,128]{3,0,2,1:T(8,128)} %get-tuple-element.293), kind=kOutput, calls=%fused_computation.3.clone.1 | convolution fusion | flops 5648147456 | bytes 19427840 | tf_op jit(solution)/shard_map/while/body/eval_jaxpr/rgjd,kgd->rgjk/dot_general | solution.py:60
  337.4 4.0 fusion.40
  341.4 12.6 %bitcast_add_fusion.3 = f32[256,4,7,128]{0,3,2,1:T(8,128)S(1)} fusion(f32[256,4,7,128]{0,3,2,1:T(8,128)S(1)} %copy-done.1, f32[512,4,128,1]{0,2,3,1:T(8,128)S(1)} %bitcast.64, f32[4,512,256,7]{2,1,3,0:T(8,128)S(1)} %get-tuple-element.259, f32[256,4,7]{0,2,1:T(8,128)S(1)} %select_maximum_fusion.2, pred[512]{0:T(512)(128)(4,1)S(1)} %dynamic-slice_compare_fusion.2, ...), kind=kOutput, calls=%fused_computation.15.clone.1 | convolution fusion | flops 5654577152 | bytes 23126528 | tf_op jit(solution)/shard_map/while/body/eval_jaxpr/rgjk,kgd->rgjd/dot_general | solution.py:68
  354.0 1.9 copy-done.2
  358.4 18.3 %bitcast_reduce_fusion.2 = (f32[256,4,7]{0,2,1:T(8,128)S(1)}, f32[4,512,256,7]{2,1,3,0:T(8,128)S(1)}) fusion(pred[512]{0:T(512)(128)(4,1)S(1)} %dynamic-slice_compare_fusion.2, f32[512,4,128,1]{0,2,3,1:T(8,128)S(1)} %bitcast.63, f32[256,4,7,128]{3,0,2,1:T(8,128)} %get-tuple-element.293), kind=kOutput, calls=%fused_computation.3.clone.1 | convolution fusion | flops 5648147456 | bytes 19427840 | tf_op jit(solution)/shard_map/while/body/eval_jaxpr/rgjd,kgd->rgjk/dot_general | solution.py:60
  376.8 4.0 fusion.40
  380.8 12.6 %bitcast_add_fusion.3 = f32[256,4,7,128]{0,3,2,1:T(8,128)S(1)} fusion(f32[256,4,7,128]{0,3,2,1:T(8,128)S(1)} %copy-done.1, f32[512,4,128,1]{0,2,3,1:T(8,128)S(1)} %bitcast.64, f32[4,512,256,7]{2,1,3,0:T(8,128)S(1)} %get-tuple-element.259, f32[256,4,7]{0,2,1:T(8,128)S(1)} %select_maximum_fusion.2, pred[512]{0:T(512)(128)(4,1)S(1)} %dynamic-slice_compare_fusion.2, ...), kind=kOutput, calls=%fused_computation.15.clone.1 | convolution fusion | flops 5654577152 | bytes 23126528 | tf_op jit(solution)/shard_map/while/body/eval_jaxpr/rgjk,kgd->rgjd/dot_general | solution.py:68
  393.5 1.9 copy-done.2
  396.3 7.3 %all-to-all-start.2 = ((f32[8,256,4,7]{1,2,3,0:T(4,128)}), f32[8,256,4,7]{1,2,3,0:T(4,128)S(1)}, u32[]{:S(2)}, u32[]{:S(2)}) async-start(f32[8,256,4,7]{1,2,3,0:T(4,128)} %broadcast_in_dim.81), calls=%async_computation.2 | async-start | bytes 458752 | tf_op jit(solution)/shard_map/all_to_all | solution.py:12
  403.6 4.6 copy.108
  408.2 2.6 all-to-all-done.2
  411.0 2.8 copy.110
  413.8 2.8 broadcast_multiply_fusion
  419.2 87.9 %all_to_all.24 = f32[8,32,4,7,129]{4,1,3,2,0:T(8,128)} all-to-all(f32[8,32,4,7,129]{4,1,3,2,0:T(8,128)S(1)} %copy.111), channel_id=1, replica_groups=mesh['grp'=16,'blk'=8] {'blk'}, dimensions={0} | all-to-all | bytes 7397376 | tf_op jit(solution)/shard_map/all_to_all | solution.py:29
  507.1 4.0 reduce_sum.35
  (83 shorter events, 20.4 us)
Async XLA Ops:
  3.1 39.6 %all-to-all-start = ((f32[128,1,16]{2,1,0:T(1,128)}), f32[128,1,16]{2,1,0:T(1,128)S(1)}, u32[]{:S(2)}, u32[]{:S(2)}) async-start(f32[128,1,16]{2,1,0:T(1,128)} %bitcast.3), calls=%async_computation | async-start | bytes 131072 | tf_op jit(solution)/shard_map/all_to_all | solution.py:112
  42.7 10.2 %copy-start.3 = (f32[32,3584]{1,0:T(8,128)S(1)}, f32[32,3584]{1,0:T(8,128)}, u32[]{:S(2)}) copy-start(f32[32,3584]{1,0:T(8,128)} %param.7) | copy-start | bytes 1376260
  42.7 175.4 %all-to-all-start.1 = ((f32[128,16,1024]{2,1,0:T(8,128)}), f32[128,16,1024]{2,1,0:T(8,128)}, u32[]{:S(2)}, u32[]{:S(2)}) async-start(f32[128,16,1024]{2,1,0:T(8,128)} %reshape.51), calls=%async_computation.1 | async-start | bytes 16777216 | tf_op jit(solution)/shard_map/all_to_all | solution.py:111
  52.9 93.3 %collective-permute-start = (f32[32,3584]{1,0:T(8,128)S(1)}, f32[32,3584]{1,0:T(8,128)S(1)}, u32[]{:S(2)}, u32[]{:S(2)}) collective-permute-start(f32[32,3584]{1,0:T(8,128)S(1)} %copy-done.3), channel_id=1, source_target_pairs={{0,1},{1,2},{2,3},{3,4},{4,5},{5,6},{6,7},{7,0},{8,9},{9,10},{10,1... | collective-permute-start | bytes 1376264 | tf_op jit(solution)/shard_map/ppermute | solution.py:122
  53.1 99.3 %collective-permute-start.4 = (f32[32,3584]{1,0:T(8,128)S(1)}, f32[32,3584]{1,0:T(8,128)S(1)}, u32[]{:S(2)}, u32[]{:S(2)}) collective-permute-start(f32[32,3584]{1,0:T(8,128)S(1)} %copy-done.3), channel_id=1, source_target_pairs={{0,7},{1,0},{2,1},{3,2},{4,3},{5,4},{6,5},{7,6},{8,15},{9,8},{10,9... | collective-permute-start | bytes 1376264 | tf_op jit(solution)/shard_map/ppermute | solution.py:124
  146.2 11.0 %collective-permute-start.1 = (f32[32,3584]{1,0:T(8,128)S(1)}, f32[32,3584]{1,0:T(8,128)S(1)}, u32[]{:S(2)}, u32[]{:S(2)}) collective-permute-start(f32[32,3584]{1,0:T(8,128)S(1)} %collective-permute-done), channel_id=1, source_target_pairs={{0,1},{1,2},{2,3},{3,4},{4,5},{5,6},{6,7},{7,0},{8,9},{9,10},{10,1... | collective-permute-start | bytes 1376264 | tf_op jit(solution)/shard_map/ppermute | solution.py:122
  152.4 4.8 copy-start.4
  152.4 7.9 %collective-permute-start.5 = (f32[32,3584]{1,0:T(8,128)S(1)}, f32[32,3584]{1,0:T(8,128)}, u32[]{:S(2)}, u32[]{:S(2)}) collective-permute-start(f32[32,3584]{1,0:T(8,128)S(1)} %collective-permute-done.4), channel_id=1, source_target_pairs={{0,7},{1,0},{2,1},{3,2},{4,3},{5,4},{6,5},{7,6},{8,15},{9,8},{10,9... | collective-permute-start | bytes 1376264 | tf_op jit(solution)/shard_map/ppermute | solution.py:124
  157.2 3.1 copy-start.5
  157.2 9.2 %collective-permute-start.2 = (f32[32,3584]{1,0:T(8,128)S(1)}, f32[32,3584]{1,0:T(8,128)}, u32[]{:S(2)}, u32[]{:S(2)}) collective-permute-start(f32[32,3584]{1,0:T(8,128)S(1)} %collective-permute-done.1), channel_id=1, source_target_pairs={{0,1},{1,2},{2,3},{3,4},{4,5},{5,6},{6,7},{7,0},{8,9},{9,10},{10,1... | collective-permute-start | bytes 1376264 | tf_op jit(solution)/shard_map/ppermute | solution.py:122
  160.3 21.8 %collective-permute-start.6 = (f32[32,3584]{1,0:T(8,128)}, f32[32,3584]{1,0:T(8,128)}, u32[]{:S(2)}, u32[]{:S(2)}) collective-permute-start(f32[32,3584]{1,0:T(8,128)} %collective-permute-done.5), channel_id=1, source_target_pairs={{0,7},{1,0},{2,1},{3,2},{4,3},{5,4},{6,5},{7,6},{8,15},{9,8},{10,9... | collective-permute-start | bytes 1376264 | tf_op jit(solution)/shard_map/ppermute | solution.py:124
  166.5 18.5 %collective-permute-start.3 = (f32[32,3584]{1,0:T(8,128)}, f32[32,3584]{1,0:T(8,128)}, u32[]{:S(2)}, u32[]{:S(2)}) collective-permute-start(f32[32,3584]{1,0:T(8,128)} %collective-permute-done.2), channel_id=1, source_target_pairs={{0,1},{1,2},{2,3},{3,4},{4,5},{5,6},{6,7},{7,0},{8,9},{9,10},{10,1... | collective-permute-start | bytes 1376264 | tf_op jit(solution)/shard_map/ppermute | solution.py:122
  168.8 8.8 %copy-start.6 = (f32[32,3584]{1,0:T(8,128)S(1)}, f32[32,3584]{1,0:T(8,128)}, u32[]{:S(2)}) copy-start(f32[32,3584]{1,0:T(8,128)} %copy-done.5) | copy-start | bytes 1376260
  258.5 4.1 copy-start.1
  275.2 1.9 copy-start.2
  297.9 4.1 copy-start.1
  314.6 1.9 copy-start.2
  337.4 4.1 copy-start.1
  354.0 1.9 copy-start.2
  376.8 4.1 copy-start.1
  393.4 1.9 copy-start.2
  396.3 14.5 %all-to-all-start.2 = ((f32[8,256,4,7]{1,2,3,0:T(4,128)}), f32[8,256,4,7]{1,2,3,0:T(4,128)S(1)}, u32[]{:S(2)}, u32[]{:S(2)}) async-start(f32[8,256,4,7]{1,2,3,0:T(4,128)} %broadcast_in_dim.81), calls=%async_computation.2 | async-start | bytes 458752 | tf_op jit(solution)/shard_map/all_to_all | solution.py:12
  413.8 3.1 copy-start
